TPU v7x, 32 devices: a whole 2x2x4 slice. The times are simulated.
32 devices in a mesh: prow: 8 (over z, y), pcol: 4 (over x, core).
Axes of the slice: x: 2, y: 2, z: 4, core: 2. Of those that a mesh axis runs over, the one named last changes fastest.
Arguments:
- b_panel: float32 [1024, 512], P('prow'), may hold values from -6 to 6
- b_rest: float32 [8192, 512], P('prow'), may hold values from -6 to 6
- u_diag: float32 [1024, 1024], P('prow', 'pcol'), as said below
- u_panel: float32 [1024, 8192], P('pcol', 'prow'), may hold values from -0.1875 to 0.1875
- l_diag: float32 [1024, 1024], P('prow', 'pcol'), as said below
- l_below: float32 [8192, 1024], P('prow', 'pcol'), may hold values from -0.09375 to 0.09375
- v_below: float32 [8192, 512], P('prow'), may hold values from -6 to 6
- pivot: int32 [1024], replicated, may hold values from 0 to 8191, as said below
Outputs:
- w_rest: float32 [8192, 512], P('prow')
- x_panel: float32 [1024, 512], P('prow')
- x_rest: float32 [8192, 512], P('prow')
Inputs may be any that keep to these rules, and one draw needn't show every extreme that they name: `pivot`: the 1024 entries are distinct, so the interchanges are disjoint. `u_diag`: upper triangular; its diagonal lies in 1 to 2. `l_diag`: lower triangular; its diagonal is one.
All inputs are finite; a program needn't handle non-finite values.
Results may differ from a plain program's by a relative error of at most 0.00007.
Values sent between devices are 32-bit elements; how exact they have to be, the bound alone decides.
A program may use at most 128 MiB of HBM per device.

v0:
```python
import functools

import jax
import jax.numpy as jnp
from jax import lax
from jax.experimental import pallas as pl
from jax.experimental.pallas import tpu as pltpu
from jax.sharding import PartitionSpec as P

F32 = jnp.float32
BF16 = jnp.bfloat16
NN = (((1,), (0,)), ((), ()))
TN = (((0,), (0,)), ((), ()))
NT = (((1,), (1,)), ((), ()))
BLOCK = 128


def split(x):
    high = x.astype(BF16)
    return high, (x - high.astype(F32)).astype(BF16)


def dot(left, right, dims):
    return lax.dot_general(left, right, dims, preferred_element_type=F32)


def dot3(left, right, dims=NN):
    (lh, ll), (rh, rl) = left, right
    return dot(lh, rh, dims) + (dot(lh, rl, dims) + dot(ll, rh, dims))


def inverse(square, upper):
    size = square.shape[0]
    row = lax.broadcasted_iota(jnp.int32, (size, size), 0)
    col = lax.broadcasted_iota(jnp.int32, (size, size), 1)
    eye = jnp.where(row == col, 1.0, 0.0)
    if upper:
        on_diag = jnp.where(row == col, square, 0.0)
        strict = jnp.where(col > row, square, 0.0) / jnp.sum(on_diag, axis=1, keepdims=True)
    else:
        strict = jnp.where(col < row, square, 0.0)
    result = eye - strict
    halves = split(strict)
    power = dot3(halves, halves)
    reach = 2
    while reach < size:
        halves = split(power)
        result = result + dot3(split(result), halves)
        reach *= 2
        if reach < size:
            power = dot3(halves, halves)
    if upper:
        result = result / jnp.sum(on_diag, axis=0, keepdims=True)
    return result


def prep_kernel(pre, u_ref, l_ref, b_ref, lb_ref, vb_ref, piv_ref, pack_ref, coup_ref, pick_ref):
    i = lax.axis_index("prow")
    j = lax.axis_index("pcol")
    cols = u_ref.shape[1]
    chunk = pick_ref.shape[1]
    mine = pl.ds(pl.multiple_of(j * chunk, chunk), chunk)
    pack_ref[:, :cols] = u_ref[...]
    pack_ref[:, cols : 2 * cols] = l_ref[...]
    pack_ref[:, 2 * cols :] = b_ref[:, mine]
    if pre:
        ratio = cols // BLOCK

        @pl.when(i // ratio == j)
        def _():
            at = pl.multiple_of((i % ratio) * BLOCK, BLOCK)
            pack_ref[:, pl.ds(at, BLOCK)] = inverse(u_ref[:, pl.ds(at, BLOCK)], True)
            pack_ref[:, pl.ds(cols + at, BLOCK)] = inverse(l_ref[:, pl.ds(at, BLOCK)], False)

    coup_ref[...] = dot3(split(vb_ref[...]), split(lb_ref[...]), TN)
    rows = vb_ref.shape[0]
    total = piv_ref.shape[1]
    local = piv_ref[...] - i * rows
    hot = jnp.where(lax.broadcasted_iota(jnp.int32, (rows, total), 0) == local, 1.0, 0.0).astype(BF16)
    part = vb_ref[:, mine]
    first, rest = split(part)
    second = (part - first.astype(F32)).astype(BF16)
    third = (part - first.astype(F32) - second.astype(F32)).astype(BF16)
    pick_ref[...] = dot(hot, first, TN) + dot(hot, second, TN) + dot(hot, third, TN)


def main_kernel(pre, n_row, n_col, g_ref, c_ref, up_ref, br_ref, vb_ref, piv_ref, wr_ref, xr_ref, uh, ul, lh, ll, bs, cs, wh, wl):
    i = lax.axis_index("prow")
    rows = g_ref.shape[1]
    cols = up_ref.shape[0] // n_col
    chunk = g_ref.shape[2] - 2 * cols
    crow = c_ref.shape[1]
    total = uh.shape[0]
    for a in range(n_row):
        for b in range(n_col):
            at = a * n_col + b
            rs = slice(a * rows, (a + 1) * rows)
            cs_ = slice(b * cols, (b + 1) * cols)
            if a * rows < (b + 1) * cols:
                uh[rs, cs_], ul[rs, cs_] = split(g_ref[at, :, :cols])
            if (a + 1) * rows > b * cols:
                lh[rs, cs_], ll[rs, cs_] = split(g_ref[at, :, cols : 2 * cols])
            bs[rs, b * chunk : (b + 1) * chunk] = g_ref[at, :, 2 * cols :]
            cs[a * crow : (a + 1) * crow, cs_] = c_ref[at]
    count = total // BLOCK
    if not pre:
        for p in range(count):
            sl = slice(p * BLOCK, (p + 1) * BLOCK)
            uh[sl, sl], ul[sl, sl] = split(inverse(uh[sl, sl].astype(F32) + ul[sl, sl].astype(F32), True))
            lh[sl, sl], ll[sl, sl] = split(inverse(lh[sl, sl].astype(F32) + ll[sl, sl].astype(F32), False))
    for p in range(count):
        first = p * BLOCK
        sl = slice(first, first + BLOCK)
        rhs = bs[sl, :].T
        if p:
            rhs = rhs - dot3((wh[:, :first], wl[:, :first]), (uh[:first, sl], ul[:first, sl]))
        out = dot3(split(rhs), (uh[sl, sl], ul[sl, sl]))
        cs[:, sl] = out - cs[:, sl]
        wh[:, sl], wl[:, sl] = split(out)
    tile = 256
    for t in range(up_ref.shape[1] // tile):
        ts = slice(t * tile, (t + 1) * tile)
        update = dot3((wh[...], wl[...]), split(up_ref[:, ts]))
        wr_ref[ts, :] = br_ref[ts, :] - update.T
    for p in reversed(range(count)):
        first = p * BLOCK
        last = first + BLOCK
        sl = slice(first, last)
        rhs = cs[:, sl]
        if last < total:
            rhs = rhs - dot3((wh[:, last:], wl[:, last:]), (lh[last:, sl], ll[last:, sl]))
        out = dot3(split(rhs), (lh[sl, sl], ll[sl, sl]))
        cs[:, sl] = out
        wh[:, sl], wl[:, sl] = split(out)
    all_rows = vb_ref.shape[0]
    for t in range(all_rows // tile):
        ts = slice(t * tile, (t + 1) * tile)
        local = piv_ref[...] - (i * all_rows + t * tile)
        hit = lax.broadcasted_iota(jnp.int32, (tile, total), 0) == local
        hot = jnp.where(hit, 1.0, 0.0)
        used = jnp.sum(hot, axis=1, keepdims=True) > 0.5
        hot = hot.astype(BF16)
        new = dot(hot, wh[...], NT) + dot(hot, wl[...], NT)
        xr_ref[ts, :] = jnp.where(used, new, vb_ref[ts, :])


def body(n_row, n_col, b_panel, b_rest, u_diag, u_panel, l_diag, l_below, v_below, pivot):
    rows, cols = u_diag.shape
    total, rhs = pivot.shape[0], b_panel.shape[1]
    chunk = rhs // n_col
    pre = rows == BLOCK
    piv = pivot[None, :]
    vm = pl.BlockSpec(memory_space=pltpu.VMEM)
    params = pltpu.CompilerParams(vmem_limit_bytes=56 << 20)
    pack, coup, pick = pl.pallas_call(
        functools.partial(prep_kernel, pre),
        out_shape=(
            jax.ShapeDtypeStruct((rows, 2 * cols + chunk), F32),
            jax.ShapeDtypeStruct((rhs, cols), F32),
            jax.ShapeDtypeStruct((total, chunk), F32),
        ),
        in_specs=[vm] * 6,
        out_specs=(vm, vm, vm),
        compiler_params=params,
    )(u_diag, l_diag, b_panel, l_below, v_below, piv)
    gathered = lax.all_gather(pack, ("prow", "pcol"), axis=0)
    upan = lax.all_gather(u_panel, "pcol", axis=0, tiled=True)
    csum = lax.psum_scatter(coup, "prow", scatter_dimension=0, tiled=True)
    call = lax.all_gather(csum, ("prow", "pcol"), axis=0)
    xsum = lax.psum_scatter(pick, "prow", scatter_dimension=0, tiled=True)
    x_panel = lax.all_gather(xsum, "pcol", axis=1, tiled=True)
    w_rest, x_rest = pl.pallas_call(
        functools.partial(main_kernel, pre, n_row, n_col),
        out_shape=(jax.ShapeDtypeStruct(b_rest.shape, F32), jax.ShapeDtypeStruct(v_below.shape, F32)),
        in_specs=[vm] * 6,
        out_specs=(vm, vm),
        scratch_shapes=[pltpu.VMEM((total, total), BF16)] * 4
        + [pltpu.VMEM((total, rhs), F32), pltpu.VMEM((rhs, total), F32)]
        + [pltpu.VMEM((rhs, total), BF16)] * 2,
        compiler_params=params,
    )(gathered, call, upan, b_rest, v_below, piv)
    return w_rest, x_panel, x_rest


def solution(mesh):
    in_specs = (
        P("prow", None),
        P("prow", None),
        P("prow", "pcol"),
        P("pcol", "prow"),
        P("prow", "pcol"),
        P("prow", "pcol"),
        P("prow", None),
        P(),
    )
    out_specs = (P("prow", None), P("prow", None), P("prow", None))
    step = functools.partial(body, mesh.shape["prow"], mesh.shape["pcol"])
    return jax.shard_map(step, mesh=mesh, in_specs=in_specs, out_specs=out_specs, check_vma=False)
```

profile of v0, /device:TPU:0, one launch (start us, length us, event | category | flops | bytes accessed | tf_op | source)
XLA Modules:
  0.0 364.4 jit_solution(3840719177970474497)
XLA Ops:
  7.2 0.0 reduce-scatter.3.cloned.1.call-start
  7.2 7.9 %shard_map.103 = (f32[128,640]{1,0:T(8,128)}, f32[512,256]{1,0:T(8,128)}, f32[1024,128]{1,0:T(8,128)}) custom-call(f32[128,256]{1,0:T(8,128)} %u_ref.1, f32[128,256]{1,0:T(8,128)} %l_ref.1, f32[128,512]{1,0:T(8,128)} %b_ref.1, f32[1024,256]{1,0:T(8,128)} %lb_ref.1, f32[1024,512]{1,0:T(8,128)} %vb_ref.3, s32[1,1024]{1,0:T(1,128)} %bitcast.5), custom_call_target="tpu_custom_call" | custom-call | tf_op jit(solution)/shard_map/pallas_call | solution.py:155
  15.2 0.0 reduce-scatter.3.cloned.1.call-update
  15.2 0.0 reduce-scatter.5.cloned.1.call-start
  15.2 0.7 reduce-scatter.5.cloned.1.call-update
  15.9 0.0 all-gather.10.cloned.1.call-start
  16.0 63.5 %reduce-scatter.3.cloned.1.call-done = f32[64,256]{1,0:T(8,128)} async-done(((f32[512,256]{1,0:T(8,128)}), f32[64,256]{1,0:T(8,128)}) %reduce-scatter.3.cloned.1.call-update) | async-done | bytes 65552 | tf_op jit(solution)/shard_map/reduce_scatter | solution.py:168
  79.5 0.0 all-gather.10.cloned.1.call-update
  79.5 0.0 all-gather.6.cloned.1.call-start
  79.6 0.5 all-gather.6.cloned.1.call-update
  80.1 0.0 all-gather.8.cloned.1.call-start
  80.1 0.5 all-gather.8.cloned.1.call-update
  80.7 64.1 %reduce-scatter.5.cloned.1.call-done = f32[128,128]{1,0:T(8,128)} async-done(((f32[1024,128]{1,0:T(8,128)}), f32[128,128]{1,0:T(8,128)}) %reduce-scatter.5.cloned.1.call-update) | async-done | bytes 65552 | tf_op jit(solution)/shard_map/reduce_scatter | solution.py:170
  144.7 6.2 %all_gather.23 = f32[128,512]{1,0:T(8,128)S(1)} all-gather(f32[128,128]{1,0:T(8,128)} %reduce-scatter.5.cloned.1.call-done), channel_id=1, replica_groups=mesh['prow'=8,'pcol'=4] {'pcol'}, dimensions={1}, use_global_device_ids=true | all-gather | bytes 327680 | tf_op jit(solution)/shard_map/all_gather | solution.py:171
  150.9 52.1 %all-gather.10.cloned.1.call-done = f32[2048,256]{1,0:T(8,128)} async-done(((f32[64,256]{1,0:T(8,128)}), f32[2048,256]{1,0:T(8,128)}) %all-gather.10.cloned.1.call-update) | async-done | bytes 2097168 | tf_op jit(solution)/shard_map/all_gather | solution.py:169
  203.0 34.8 %all-gather.6.cloned.1.call-done.up_ref = f32[1024,1024]{1,0:T(8,128)} async-done(((f32[256,1024]{1,0:T(8,128)}), f32[1024,1024]{1,0:T(8,128)}) %all-gather.6.cloned.1.call-update) | async-done | bytes 4194320 | tf_op jit(solution)/shard_map/all_gather | solution.py:167
  237.8 89.5 %all-gather.8.cloned.1.call-done = f32[4096,640]{1,0:T(8,128)} async-done(((f32[128,640]{1,0:T(8,128)}), f32[4096,640]{1,0:T(8,128)}) %all-gather.8.cloned.1.call-update) | async-done | bytes 10485776 | tf_op jit(solution)/shard_map/all_gather | solution.py:166
  327.3 29.9 %shard_map.104 = (f32[1024,512]{1,0:T(8,128)}, f32[1024,512]{1,0:T(8,128)}) custom-call(f32[32,128,640]{2,1,0:T(8,128)} %bitcast.3, f32[32,64,256]{2,1,0:T(8,128)} %bitcast.4, f32[1024,1024]{1,0:T(8,128)} %all-gather.6.cloned.1.call-done.up_ref, f32[1024,512]{1,0:T(8,128)} %br_ref.1, f32[1024,512]{1,0:T(8,128)} %vb_ref.3, s32[1,1024]{1,0:T(1,128)} %bitcast.6), custom_call_target="tpu_custom_call" | custom-call | tf_op jit(solution)/shard_map/pallas_call | solution.py:172
  357.2 0.7 copy.12
Async XLA Ops:
  7.2 72.3 %reduce-scatter.3.cloned.1.call-start = ((), (), s32[]{:S(2)}) async-start(), calls=%async_computation.2 | async-start | bytes 589824 | tf_op jit(solution)/shard_map/reduce_scatter | solution.py:168
  15.2 129.6 %reduce-scatter.5.cloned.1.call-start = ((), (), s32[]{:S(2)}) async-start(), calls=%async_computation.4 | async-start | bytes 589824 | tf_op jit(solution)/shard_map/reduce_scatter | solution.py:170
  15.9 187.1 %all-gather.10.cloned.1.call-start = ((), (), s32[]{:S(2)}) async-start(), calls=%async_computation.6 | async-start | bytes 2162688 | tf_op jit(solution)/shard_map/all_gather | solution.py:169
  79.5 158.3 %all-gather.6.cloned.1.call-start = ((), (), s32[]{:S(2)}) async-start(), calls=%async_computation.3 | async-start | bytes 5242880 | tf_op jit(solution)/shard_map/all_gather | solution.py:167
  80.1 247.2 %all-gather.8.cloned.1.call-start = ((), (), s32[]{:S(2)}) async-start(), calls=%async_computation.5 | async-start | bytes 10813440 | tf_op jit(solution)/shard_map/all_gather | solution.py:166
Sparse Core Ops, SparseCore 0:
  15.3 64.1 reduce-scatter.2
  83.8 60.9 reduce-scatter.4
  147.6 55.3 all-gather.9
  204.4 33.3 all-gather.5
  240.5 86.7 all-gather.7
where the time goes:
time: 365 us; the launch traced here: 364 us
  waiting for transfers between devices  306 us (84%)
  Pallas kernels  37.9 us (10%)
  between operations  13.8 us (4%)
  blocking collectives  6.16 us (2%)
    all_gather x1, waiting for transfers between devices, body(): gathered = lax.all_gather(pack, ('prow', 'pcol'), axis=0)  89.5 us
    reduce_scatter x1, waiting for transfers between devices, body(): xsum = lax.psum_scatter(pick, 'prow', scatter_dimension=0, tiled=True)  64.1 us
    reduce_scatter x1, waiting for transfers between devices, body(): csum = lax.psum_scatter(coup, 'prow', scatter_dimension=0, tiled=True)  63.5 us
    all_gather x1, waiting for transfers between devices, body(): call = lax.all_gather(csum, ('prow', 'pcol'), axis=0)  52.1 us
    all_gather x1, waiting for transfers between devices, body(): upan = lax.all_gather(u_panel, 'pcol', axis=0, tiled=True)  34.8 us
    pallas_call x1, Pallas kernels, body(): pl.pallas_call(functools.partial(main_kernel, pre, n_row, n_col), out_sha...  29.9 us
    pallas_call x1, Pallas kernels, body(): pl.pallas_call(functools.partial(prep_kernel, pre), out_shape=(jax.ShapeD...  7.95 us
  transfers between devices with their start and end apart: 5, of which 5 were waited for; matrix products, arithmetic and copies ran while one was open for 0% of the time, Pallas kernels for 0%

commit v1 on v0

--- a/solution.py
+++ b/solution.py
@@ -13,6 +13,7 @@
 TN = (((0,), (0,)), ((), ()))
 NT = (((1,), (1,)), ((), ()))
 BLOCK = 128
+MESH = pl.DeviceIdType.MESH
 
 
 def split(x):
@@ -54,23 +55,23 @@
     return result
 
 
-def prep_kernel(pre, u_ref, l_ref, b_ref, lb_ref, vb_ref, piv_ref, pack_ref, coup_ref, pick_ref):
+def prep_kernel(pre, u_ref, l_ref, b_ref, lb_ref, vb_ref, piv_ref, pack_ref, extra_ref, coup_ref, pick_ref):
     i = lax.axis_index("prow")
     j = lax.axis_index("pcol")
     cols = u_ref.shape[1]
     chunk = pick_ref.shape[1]
     mine = pl.ds(pl.multiple_of(j * chunk, chunk), chunk)
-    pack_ref[:, :cols] = u_ref[...]
-    pack_ref[:, cols : 2 * cols] = l_ref[...]
-    pack_ref[:, 2 * cols :] = b_ref[:, mine]
+    ratio = cols // u_ref.shape[0]
+    pack_ref[:, :cols] = jnp.where(i // ratio > j, l_ref[...], u_ref[...])
+    pack_ref[:, cols:] = b_ref[:, mine]
+    extra_ref[...] = l_ref[...]
     if pre:
-        ratio = cols // BLOCK
 
         @pl.when(i // ratio == j)
         def _():
             at = pl.multiple_of((i % ratio) * BLOCK, BLOCK)
             pack_ref[:, pl.ds(at, BLOCK)] = inverse(u_ref[:, pl.ds(at, BLOCK)], True)
-            pack_ref[:, pl.ds(cols + at, BLOCK)] = inverse(l_ref[:, pl.ds(at, BLOCK)], False)
+            extra_ref[:, pl.ds(at, BLOCK)] = inverse(l_ref[:, pl.ds(at, BLOCK)], False)
 
     coup_ref[...] = dot3(split(vb_ref[...]), split(lb_ref[...]), TN)
     rows = vb_ref.shape[0]
@@ -84,11 +85,177 @@
     pick_ref[...] = dot(hot, first, TN) + dot(hot, second, TN) + dot(hot, third, TN)
 
 
-def main_kernel(pre, n_row, n_col, g_ref, c_ref, up_ref, br_ref, vb_ref, piv_ref, wr_ref, xr_ref, uh, ul, lh, ll, bs, cs, wh, wl):
+def comm_kernel(n, m, m_ref, e_ref, coup_ref, pick_ref, up_ref, gm, ge, gc, gu, xp, cslots, xslots, xparts,
+                ring_s, ring_r, side_s, side_r, cross_s, cross_r, sum_s, sum_r, pick_s, pick_r, x_s, x_r, up_s, up_r):
+    i = lax.axis_index("prow")
+    j = lax.axis_index("pcol")
+    half = n // 2
+    rows, cols = e_ref.shape
+    ratio = cols // rows
+    crow = cslots.shape[1]
+    odd = i % 2
+    pos = odd * (n - 1 - i // 2) + (1 - odd) * (i // 2)
+
+    def member(at):
+        at = (at + n) % n
+        back = at // half
+        return (1 - back) * 2 * at + back * (2 * (n - 1 - at) + 1)
+
+    right, left = member(pos + 1), member(pos - 1)
+    across = (j + m // 2) % m
+    beside = j + 1 - 2 * (j % 2)
+    owners = (j, across)
+    guests = (beside, (beside + m // 2) % m)
+    parity = j % 2
+
+    barrier = pltpu.get_barrier_semaphore()
+    for d in range(1, n):
+        pl.semaphore_signal(barrier, inc=1, device_id=((i + d) % n, j), device_id_type=MESH)
+    for d in range(1, m):
+        pl.semaphore_signal(barrier, inc=1, device_id=(i, (j + d) % m), device_id_type=MESH)
+    pl.semaphore_wait(barrier, n + m - 2)
+
+    pending = []
+
+    def guard(cond, action):
+        if cond is None:
+            action()
+        else:
+            pl.when(cond)(action)
+
+    def both(one, two):
+        if one is None or two is None:
+            return two if one is None else one
+        return one & two
+
+    def send(src, dst, s_sem, r_sem, to, cond=None):
+        copy = pltpu.make_async_remote_copy(src_ref=src, dst_ref=dst, send_sem=s_sem, recv_sem=r_sem, device_id=to, device_id_type=MESH)
+        guard(cond, copy.start)
+        pending.append((cond, copy))
+
+    def receive(dst, s_sem, r_sem, frm, cond=None):
+        copy = pltpu.make_async_remote_copy(src_ref=dst, dst_ref=dst, send_sem=s_sem, recv_sem=r_sem, device_id=frm, device_id_type=MESH)
+        guard(cond, copy.wait_recv)
+
+    bufs = (gm, ge, gc)
+
+    def needed(t, row, col):
+        return row // ratio == col if t == 1 else None
+
+    def reach(way, hop, par):
+        if hop < half:
+            return None
+        return par == way
+
+    def emit(t, k):
+        col = owners[k]
+        slot = bufs[t].at[i, col]
+        cond = needed(t, i, col)
+        for way, to in ((0, right), (1, left)):
+            send(slot, slot, ring_s.at[t, k, way, 0], ring_r.at[t, k, way, 0], (to, j), cond)
+        send(slot, slot, side_s.at[t, k, 0, 0], side_r.at[t, k, 0, 0], (i, beside), cond)
+
+    def advance(t, k, hop):
+        col = owners[k]
+        for way, to, frm in ((0, right, left), (1, left, right)):
+            row = member(pos - hop) if way == 0 else member(pos + hop)
+            slot = bufs[t].at[row, col]
+            cond = both(needed(t, row, col), reach(way, hop, parity))
+            receive(slot, ring_s.at[t, k, way, hop - 1], ring_r.at[t, k, way, hop - 1], (frm, j), cond)
+            if hop < half:
+                onward = both(needed(t, row, col), reach(way, hop + 1, parity))
+                send(slot, slot, ring_s.at[t, k, way, hop], ring_r.at[t, k, way, hop], (to, j), onward)
+            send(slot, slot, side_s.at[t, k, way, hop], side_r.at[t, k, way, hop], (i, beside), cond)
+
+    def side_arrivals(t, k):
+        col = guests[k]
+        for hop in range(half + 1):
+            for way in (0, 1):
+                if hop == 0 and way == 1:
+                    continue
+                row = i if hop == 0 else (member(pos - hop) if way == 0 else member(pos + hop))
+                limit = None if hop == 0 else reach(way, hop, 1 - parity)
+                receive(bufs[t].at[row, col], side_s.at[t, k, way, hop], side_r.at[t, k, way, hop], (i, beside), both(needed(t, row, col), limit))
+
+    def exchange(t):
+        slot = bufs[t].at[i, j]
+        send(slot, slot, cross_s.at[t], cross_r.at[t], (i, across), needed(t, i, j))
+
+    def exchanged(t):
+        receive(bufs[t].at[i, across], cross_s.at[t], cross_r.at[t], (i, across), needed(t, i, across))
+
+    gm[i, j] = m_ref[...]
+    ge[i, j] = e_ref[...]
+    exchange(0)
+    exchange(1)
+    emit(0, 0)
+    emit(1, 0)
+    for d in range(1, n):
+        to = (i + d) % n
+        send(coup_ref.at[pl.ds(to * crow, crow)], cslots.at[d - 1], sum_s.at[d - 1], sum_r.at[d - 1], (to, j))
+    gu[j] = up_ref[...]
+    send(gu.at[j], gu.at[j], up_s.at[0], up_r.at[0], (i, across))
+    send(gu.at[j], gu.at[j], up_s.at[1], up_r.at[1], (i, beside))
+    exchanged(0)
+    exchanged(1)
+    emit(0, 1)
+    emit(1, 1)
+    for t in (0, 1):
+        for k in (0, 1):
+            advance(t, k, 1)
+    total = coup_ref[pl.ds(i * crow, crow), :]
+    for d in range(1, n):
+        receive(cslots.at[d - 1], sum_s.at[d - 1], sum_r.at[d - 1], ((i - d + n) % n, j))
+        total = total + cslots[d - 1]
+    gc[i, j] = total
+    exchange(2)
+    emit(2, 0)
+    for t in (0, 1):
+        for k in (0, 1):
+            advance(t, k, 2)
+    exchanged(2)
+    emit(2, 1)
+    for d in range(1, n):
+        to = (i + d) % n
+        send(pick_ref.at[pl.ds(to * rows, rows)], xslots.at[d - 1], pick_s.at[d - 1], pick_r.at[d - 1], (to, j))
+    for hop in range(3, half + 2):
+        for t in (0, 1, 2):
+            for k in (0, 1):
+                if t == 2:
+                    advance(t, k, hop - 2)
+                elif hop <= half:
+                    advance(t, k, hop)
+    for k in (0, 1):
+        advance(2, k, half)
+    receive(gu.at[across], up_s.at[0], up_r.at[0], (i, across))
+    send(gu.at[across], gu.at[across], up_s.at[2], up_r.at[2], (i, beside))
+    own = pick_ref[pl.ds(i * rows, rows), :]
+    for d in range(1, n):
+        receive(xslots.at[d - 1], pick_s.at[d - 1], pick_r.at[d - 1], ((i - d + n) % n, j))
+        own = own + xslots[d - 1]
+    xparts[j] = own
+    for d in range(1, m):
+        send(xparts.at[j], xparts.at[j], x_s.at[d - 1], x_r.at[d - 1], (i, (j + d) % m))
+    for t in (0, 1, 2):
+        for k in (0, 1):
+            side_arrivals(t, k)
+    receive(gu.at[beside], up_s.at[1], up_r.at[1], (i, beside))
+    receive(gu.at[guests[1]], up_s.at[2], up_r.at[2], (i, beside))
+    chunk = xparts.shape[2]
+    for d in range(1, m):
+        frm = (j - d + m) % m
+        receive(xparts.at[frm], x_s.at[d - 1], x_r.at[d - 1], (i, frm))
+    for q in range(m):
+        xp[:, q * chunk : (q + 1) * chunk] = xparts[q]
+    for cond, copy in pending:
+        guard(cond, copy.wait_send)
+
+
+def main_kernel(pre, n_row, n_col, g_ref, e_ref, c_ref, up_ref, br_ref, vb_ref, piv_ref, wr_ref, xr_ref, uh, ul, lh, ll, bs, cs, wh, wl):
     i = lax.axis_index("prow")
     rows = g_ref.shape[1]
     cols = up_ref.shape[0] // n_col
-    chunk = g_ref.shape[2] - 2 * cols
+    chunk = g_ref.shape[2] - cols
     crow = c_ref.shape[1]
     total = uh.shape[0]
     for a in range(n_row):
@@ -96,11 +263,14 @@
             at = a * n_col + b
             rs = slice(a * rows, (a + 1) * rows)
             cs_ = slice(b * cols, (b + 1) * cols)
-            if a * rows < (b + 1) * cols:
+            place = a // (cols // rows)
+            if place <= b:
                 uh[rs, cs_], ul[rs, cs_] = split(g_ref[at, :, :cols])
-            if (a + 1) * rows > b * cols:
-                lh[rs, cs_], ll[rs, cs_] = split(g_ref[at, :, cols : 2 * cols])
-            bs[rs, b * chunk : (b + 1) * chunk] = g_ref[at, :, 2 * cols :]
+            if place == b:
+                lh[rs, cs_], ll[rs, cs_] = split(e_ref[at])
+            if place > b:
+                lh[rs, cs_], ll[rs, cs_] = split(g_ref[at, :, :cols])
+            bs[rs, b * chunk : (b + 1) * chunk] = g_ref[at, :, cols:]
             cs[a * crow : (a + 1) * crow, cs_] = c_ref[at]
     count = total // BLOCK
     if not pre:
@@ -152,33 +322,75 @@
     piv = pivot[None, :]
     vm = pl.BlockSpec(memory_space=pltpu.VMEM)
     params = pltpu.CompilerParams(vmem_limit_bytes=56 << 20)
-    pack, coup, pick = pl.pallas_call(
+    pack, extra, coup, pick = pl.pallas_call(
         functools.partial(prep_kernel, pre),
         out_shape=(
-            jax.ShapeDtypeStruct((rows, 2 * cols + chunk), F32),
+            jax.ShapeDtypeStruct((rows, cols + chunk), F32),
+            jax.ShapeDtypeStruct((rows, cols), F32),
             jax.ShapeDtypeStruct((rhs, cols), F32),
             jax.ShapeDtypeStruct((total, chunk), F32),
         ),
         in_specs=[vm] * 6,
-        out_specs=(vm, vm, vm),
+        out_specs=(vm,) * 4,
         compiler_params=params,
     )(u_diag, l_diag, b_panel, l_below, v_below, piv)
-    gathered = lax.all_gather(pack, ("prow", "pcol"), axis=0)
-    upan = lax.all_gather(u_panel, "pcol", axis=0, tiled=True)
-    csum = lax.psum_scatter(coup, "prow", scatter_dimension=0, tiled=True)
-    call = lax.all_gather(csum, ("prow", "pcol"), axis=0)
-    xsum = lax.psum_scatter(pick, "prow", scatter_dimension=0, tiled=True)
-    x_panel = lax.all_gather(xsum, "pcol", axis=1, tiled=True)
+    if n_row == 8 and n_col == 4:
+        crow, half = rhs // n_row, n_row // 2
+        dma = pltpu.SemaphoreType.DMA
+        gm, ge, gc, gu, x_panel = pl.pallas_call(
+            functools.partial(comm_kernel, n_row, n_col),
+            out_shape=(
+                jax.ShapeDtypeStruct((n_row, n_col, rows, cols + chunk), F32),
+                jax.ShapeDtypeStruct((n_row, n_col, rows, cols), F32),
+                jax.ShapeDtypeStruct((n_row, n_col, crow, cols), F32),
+                jax.ShapeDtypeStruct((n_col,) + u_panel.shape, F32),
+                jax.ShapeDtypeStruct((rows, rhs), F32),
+            ),
+            in_specs=[vm] * 5,
+            out_specs=(vm,) * 5,
+            scratch_shapes=[
+                pltpu.VMEM((n_row - 1, crow, cols), F32),
+                pltpu.VMEM((n_row - 1, rows, chunk), F32),
+                pltpu.VMEM((n_col, rows, chunk), F32),
+                dma((3, 2, 2, half)),
+                dma((3, 2, 2, half)),
+                dma((3, 2, 2, half + 1)),
+                dma((3, 2, 2, half + 1)),
+                dma((3,)),
+                dma((3,)),
+                dma((n_row - 1,)),
+                dma((n_row - 1,)),
+                dma((n_row - 1,)),
+                dma((n_row - 1,)),
+                dma((n_col - 1,)),
+                dma((n_col - 1,)),
+                dma((3,)),
+                dma((3,)),
+            ],
+            compiler_params=pltpu.CompilerParams(vmem_limit_bytes=56 << 20, collective_id=0, has_side_effects=True),
+        )(pack, extra, coup, pick, u_panel)
+        gathered = gm.reshape(n_row * n_col, rows, cols + chunk)
+        extras = ge.reshape(n_row * n_col, rows, cols)
+        call = gc.reshape(n_row * n_col, crow, cols)
+        upan = gu.reshape(n_col * u_panel.shape[0], u_panel.shape[1])
+    else:
+        gathered = lax.all_gather(pack, ("prow", "pcol"), axis=0)
+        extras = lax.all_gather(extra, ("prow", "pcol"), axis=0)
+        upan = lax.all_gather(u_panel, "pcol", axis=0, tiled=True)
+        csum = lax.psum_scatter(coup, "prow", scatter_dimension=0, tiled=True)
+        call = lax.all_gather(csum, ("prow", "pcol"), axis=0)
+        xsum = lax.psum_scatter(pick, "prow", scatter_dimension=0, tiled=True)
+        x_panel = lax.all_gather(xsum, "pcol", axis=1, tiled=True)
     w_rest, x_rest = pl.pallas_call(
         functools.partial(main_kernel, pre, n_row, n_col),
         out_shape=(jax.ShapeDtypeStruct(b_rest.shape, F32), jax.ShapeDtypeStruct(v_below.shape, F32)),
-        in_specs=[vm] * 6,
+        in_specs=[vm] * 7,
         out_specs=(vm, vm),
         scratch_shapes=[pltpu.VMEM((total, total), BF16)] * 4
         + [pltpu.VMEM((total, rhs), F32), pltpu.VMEM((rhs, total), F32)]
         + [pltpu.VMEM((rhs, total), BF16)] * 2,
         compiler_params=params,
-    )(gathered, call, upan, b_rest, v_below, piv)
+    )(gathered, extras, call, upan, b_rest, v_below, piv)
     return w_rest, x_panel, x_rest
 
 

time: 365 us -> 130 us (0.36)
  waiting for transfers between devices: 306 us -> 0 us
  Pallas kernels: 37.9 us -> 128 us
  between operations: 13.8 us -> 0.65 us
  blocking collectives: 6.16 us -> 0 us
    all_gather x3 -> x0, waiting for transfers between devices: 176 us -> none  [the longest x1 89.5 us: body(): gathered = lax.all_gather(pack, ('prow', 'pcol'), axis=0)]
    reduce_scatter x2 -> x0, waiting for transfers between devices: 128 us -> none  [the longest x1 64.1 us: body(): xsum = lax.psum_scatter(pick, 'prow', scatter_dimension=0, tiled=True)]
    pallas_call x0 -> x1, Pallas kernels: none -> 90.2 us  [body(): pl.pallas_call(functools.partial(comm_kernel, n_row, n_col), out_shape=(j...]
    all_gather x1 -> x0, blocking collectives: 6.16 us -> none  [body(): x_panel = lax.all_gather(xsum, 'pcol', axis=1, tiled=True)]
  transfers between devices with their start and end apart: 5 -> 0, of which waited for: 5 -> 0; matrix products, arithmetic and copies ran while one was open for 0% -> 0% of each run, Pallas kernels for 0% -> 0%
where the time goes in v1:
time: 130 us; the launch traced here: 129 us
  Pallas kernels  128 us (98%)
    pallas_call x1, Pallas kernels, body(): pl.pallas_call(functools.partial(comm_kernel, n_row, n_col), out_shape=(j...  90.2 us
    pallas_call x1, Pallas kernels, body(): pl.pallas_call(functools.partial(main_kernel, pre, n_row, n_col), out_sha...  29.9 us
    pallas_call x1, Pallas kernels, body(): pl.pallas_call(functools.partial(prep_kernel, pre), out_shape=(jax.ShapeD...  7.95 us

profile of v1, /device:TPU:0, one launch (start us, length us, event | category | flops | bytes accessed | tf_op | source)
XLA Modules:
  0.0 129.5 jit_solution(14499809315565960373)
XLA Ops:
  0.6 7.9 %shard_map.103 = (f32[128,384]{1,0:T(8,128)}, f32[128,256]{1,0:T(8,128)}, f32[512,256]{1,0:T(8,128)}, f32[1024,128]{1,0:T(8,128)}) custom-call(f32[128,256]{1,0:T(8,128)} %u_ref.1, f32[128,256]{1,0:T(8,128)} %l_ref.1, f32[128,512]{1,0:T(8,128)} %b_ref.1, f32[1024,256]{1,0:T(8,128)} %lb_ref.1, f32[1024,512]{1,0:T(8,128)} %vb_ref.3, s32[1,1024]{1,0:T(1,128)} %bitcast.9), custom_call_target="tpu_custom_call" | custom-call | tf_op jit(solution)/shard_map/pallas_call | solution.py:325
  8.6 90.2 %shard_map.104 = (f32[8,4,128,384]{3,2,1,0:T(8,128)}, f32[8,4,128,256]{3,2,1,0:T(8,128)}, f32[8,4,64,256]{3,2,1,0:T(8,128)}, f32[4,256,1024]{2,1,0:T(8,128)}, f32[128,512]{1,0:T(8,128)}) custom-call(f32[128,384]{1,0:T(8,128)} %get-tuple-element.14.m_ref, f32[128,256]{1,0:T(8,128)} %get-tuple-element.15.e_ref, f32[512,256]{1,0:T(8,128)} %get-tuple-element.16.coup_ref, ...), custom_call_target="tpu_custom_call" | custom-call | tf_op jit(solution)/shard_map/pallas_call | solution.py:340
  98.8 0.0 copy-start
  98.8 29.9 %shard_map.105 = (f32[1024,512]{1,0:T(8,128)}, f32[1024,512]{1,0:T(8,128)}) custom-call(f32[32,128,384]{2,1,0:T(8,128)} %bitcast.5, f32[32,128,256]{2,1,0:T(8,128)} %bitcast.6, f32[32,64,256]{2,1,0:T(8,128)} %bitcast.8, f32[1024,1024]{1,0:T(8,128)} %bitcast.7, f32[1024,512]{1,0:T(8,128)} %br_ref.1, f32[1024,512]{1,0:T(8,128)} %vb_ref.3, s32[1,1024]{1,0:T(1,128)} %bitcast.10), custom_call_target="tpu_custom_call" | custom-call | tf_op jit(solution)/shard_map/pallas_call | solution.py:384
  128.8 0.0 copy-done
  128.8 0.7 copy.12
Async XLA Ops:
  98.8 29.9 %copy-start = (f32[128,512]{1,0:T(8,128)S(1)}, f32[128,512]{1,0:T(8,128)}, u32[]{:S(2)}) copy-start(f32[128,512]{1,0:T(8,128)} %get-tuple-element.29) | copy-start | bytes 786436

commit v2 on v1

v2 whole, which is shorter than its diff:
```python
import functools

import jax
import jax.numpy as jnp
from jax import lax
from jax.experimental import pallas as pl
from jax.experimental.pallas import tpu as pltpu
from jax.sharding import PartitionSpec as P

F32 = jnp.float32
BF16 = jnp.bfloat16
NN = (((1,), (0,)), ((), ()))
TN = (((0,), (0,)), ((), ()))
NT = (((1,), (1,)), ((), ()))
BLOCK = 128
MESH = pl.DeviceIdType.MESH


def split(x):
    high = x.astype(BF16)
    return high, (x - high.astype(F32)).astype(BF16)


def dot(left, right, dims):
    return lax.dot_general(left, right, dims, preferred_element_type=F32)


def dot3(left, right, dims=NN):
    (lh, ll), (rh, rl) = left, right
    return dot(lh, rh, dims) + (dot(lh, rl, dims) + dot(ll, rh, dims))


def inverse(square, upper):
    size = square.shape[0]
    row = lax.broadcasted_iota(jnp.int32, (size, size), 0)
    col = lax.broadcasted_iota(jnp.int32, (size, size), 1)
    eye = jnp.where(row == col, 1.0, 0.0)
    if upper:
        on_diag = jnp.where(row == col, square, 0.0)
        strict = jnp.where(col > row, square, 0.0) / jnp.sum(on_diag, axis=1, keepdims=True)
    else:
        strict = jnp.where(col < row, square, 0.0)
    result = eye - strict
    halves = split(strict)
    power = dot3(halves, halves)
    reach = 2
    while reach < size:
        halves = split(power)
        result = result + dot3(split(result), halves)
        reach *= 2
        if reach < size:
            power = dot3(halves, halves)
    if upper:
        result = result / jnp.sum(on_diag, axis=0, keepdims=True)
    return result


def prep_kernel(pre, u_ref, l_ref, b_ref, lb_ref, vb_ref, piv_ref, pack_ref, extra_ref, coup_ref, pick_ref):
    i = lax.axis_index("prow")
    j = lax.axis_index("pcol")
    cols = u_ref.shape[1]
    chunk = pick_ref.shape[1]
    mine = pl.ds(pl.multiple_of(j * chunk, chunk), chunk)
    ratio = cols // u_ref.shape[0]
    pack_ref[:, :cols] = jnp.where(i // ratio > j, l_ref[...], u_ref[...])
    pack_ref[:, cols:] = b_ref[:, mine]
    extra_ref[...] = l_ref[...]
    if pre:

        @pl.when(i // ratio == j)
        def _():
            at = pl.multiple_of((i % ratio) * BLOCK, BLOCK)
            pack_ref[:, pl.ds(at, BLOCK)] = inverse(u_ref[:, pl.ds(at, BLOCK)], True)
            extra_ref[:, pl.ds(at, BLOCK)] = inverse(l_ref[:, pl.ds(at, BLOCK)], False)

    coup_ref[...] = dot3(split(vb_ref[...]), split(lb_ref[...]), TN)
    pick_rows(i, vb_ref, piv_ref, pick_ref, mine)


def pick_rows(i, vb_ref, piv_ref, pick_ref, mine):
    rows = vb_ref.shape[0]
    total = piv_ref.shape[1]
    local = piv_ref[...] - i * rows
    hot = jnp.where(lax.broadcasted_iota(jnp.int32, (rows, total), 0) == local, 1.0, 0.0).astype(BF16)
    part = vb_ref[:, mine]
    first, _ = split(part)
    second = (part - first.astype(F32)).astype(BF16)
    third = (part - first.astype(F32) - second.astype(F32)).astype(BF16)
    pick_ref[...] = dot(hot, first, TN) + dot(hot, second, TN) + dot(hot, third, TN)


def assemble(n_row, n_col, g_ref, e_ref, uh, ul, lh, ll, bs):
    rows, cols = e_ref.shape[2:]
    chunk = g_ref.shape[3] - cols
    for a in range(n_row):
        for b in range(n_col):
            rs = slice(a * rows, (a + 1) * rows)
            cs_ = slice(b * cols, (b + 1) * cols)
            place = a // (cols // rows)
            if place <= b:
                uh[rs, cs_], ul[rs, cs_] = split(g_ref[a, b, :, :cols])
            if place == b:
                lh[rs, cs_], ll[rs, cs_] = split(e_ref[a, b])
            if place > b:
                lh[rs, cs_], ll[rs, cs_] = split(g_ref[a, b, :, :cols])
            bs[rs, b * chunk : (b + 1) * chunk] = g_ref[a, b, :, cols:]


def first_solve(bs, cs, wh, wl, uh, ul, service):
    for p in range(bs.shape[0] // BLOCK):
        first = p * BLOCK
        sl = slice(first, first + BLOCK)
        rhs = bs[sl, :].T
        if p:
            rhs = rhs - dot3((wh[:, :first], wl[:, :first]), (uh[:first, sl], ul[:first, sl]))
        out = dot3(split(rhs), (uh[sl, sl], ul[sl, sl]))
        cs[:, sl] = out
        wh[:, sl], wl[:, sl] = split(out)
        service(p)


def rest_update(wh, wl, columns, br_ref, wr_ref):
    tile = 256
    for t in range(wr_ref.shape[0] // tile):
        ts = slice(t * tile, (t + 1) * tile)
        wr_ref[ts, :] = br_ref[ts, :] - dot3((wh[...], wl[...]), split(columns(ts))).T


def second_solve(cs, wh, wl, lh, ll):
    total = cs.shape[1]
    for p in reversed(range(total // BLOCK)):
        last = (p + 1) * BLOCK
        sl = slice(p * BLOCK, last)
        rhs = cs[:, sl]
        if last < total:
            rhs = rhs - dot3((wh[:, last:], wl[:, last:]), (lh[last:, sl], ll[last:, sl]))
        wh[:, sl], wl[:, sl] = split(dot3(split(rhs), (lh[sl, sl], ll[sl, sl])))


def interchange(i, wh, wl, vb_ref, piv_ref, xr_ref):
    tile = 256
    all_rows, total = vb_ref.shape[0], piv_ref.shape[1]
    for t in range(all_rows // tile):
        ts = slice(t * tile, (t + 1) * tile)
        local = piv_ref[...] - (i * all_rows + t * tile)
        hot = jnp.where(lax.broadcasted_iota(jnp.int32, (tile, total), 0) == local, 1.0, 0.0)
        used = jnp.sum(hot, axis=1, keepdims=True) > 0.5
        hot = hot.astype(BF16)
        new = dot(hot, wh[...], NT) + dot(hot, wl[...], NT)
        xr_ref[ts, :] = jnp.where(used, new, vb_ref[ts, :])


def whole_kernel(n, m, u_ref, l_ref, b_ref, lb_ref, vb_ref, piv_ref, up_ref, br_ref, wr_ref, xr_ref, xp,
                 gm, ge, gc, gu, coup_ref, pick_ref, uh, ul, lh, ll, bs, cs, wh, wl, cslots, xslots, xparts,
                 ring_s, ring_r, side_s, side_r, cross_s, cross_r, sum_s, sum_r, pick_s, pick_r, x_s, x_r, up_s, up_r, late_s, late_r):
    i = lax.axis_index("prow")
    j = lax.axis_index("pcol")
    half = n // 2
    rows, cols = u_ref.shape
    ratio = cols // rows
    crow = cslots.shape[1]
    odd = i % 2
    pos = odd * (n - 1 - i // 2) + (1 - odd) * (i // 2)

    def member(at):
        at = (at + n) % n
        back = at // half
        return (1 - back) * 2 * at + back * (2 * (n - 1 - at) + 1)

    right, left = member(pos + 1), member(pos - 1)
    across = (j + m // 2) % m
    beside = j + 1 - 2 * (j % 2)
    owners = (j, across)
    guests = (beside, (beside + m // 2) % m)
    parity = j % 2

    barrier = pltpu.get_barrier_semaphore()
    for d in range(1, n):
        pl.semaphore_signal(barrier, inc=1, device_id=((i + d) % n, j), device_id_type=MESH)
    for d in range(1, m):
        pl.semaphore_signal(barrier, inc=1, device_id=(i, (j + d) % m), device_id_type=MESH)

    pending = []

    def guard(cond, action):
        if cond is None:
            action()
        else:
            pl.when(cond)(action)

    def both(one, two):
        if one is None or two is None:
            return two if one is None else one
        return one & two

    def send(src, dst, s_sem, r_sem, to, cond=None):
        copy = pltpu.make_async_remote_copy(src_ref=src, dst_ref=dst, send_sem=s_sem, recv_sem=r_sem, device_id=to, device_id_type=MESH)
        guard(cond, copy.start)
        pending.append((cond, copy))

    def receive(dst, s_sem, r_sem, frm, cond=None):
        copy = pltpu.make_async_remote_copy(src_ref=dst, dst_ref=dst, send_sem=s_sem, recv_sem=r_sem, device_id=frm, device_id_type=MESH)
        guard(cond, copy.wait_recv)

    bufs = (gm, ge, gc)

    def needed(t, row, col):
        return row // ratio == col if t == 1 else None

    def reach(way, hop, par):
        if hop < half:
            return None
        return par == way

    def emit(t, k):
        col = owners[k]
        slot = bufs[t].at[i, col]
        cond = needed(t, i, col)
        for way, to in ((0, right), (1, left)):
            send(slot, slot, ring_s.at[t, k, way, 0], ring_r.at[t, k, way, 0], (to, j), cond)
        send(slot, slot, side_s.at[t, k, 0, 0], side_r.at[t, k, 0, 0], (i, beside), cond)
        if t == 2:
            send(slot, slot, late_s.at[0, 0], late_r.at[0, 0], (i, across))

    def crossed(hop):
        for way in (0, 1) if hop else (0,):
            row = member(pos - hop) if way == 0 else member(pos + hop)
            slot = gc.at[row, across]
            cond = reach(way, hop, parity)
            receive(slot, late_s.at[way, hop], late_r.at[way, hop], (i, across), cond)
            send(slot, slot, side_s.at[2, 1, way, hop], side_r.at[2, 1, way, hop], (i, beside), cond)

    def advance(t, k, hop):
        col = owners[k]
        for way, to, frm in ((0, right, left), (1, left, right)):
            row = member(pos - hop) if way == 0 else member(pos + hop)
            slot = bufs[t].at[row, col]
            cond = both(needed(t, row, col), reach(way, hop, parity))
            receive(slot, ring_s.at[t, k, way, hop - 1], ring_r.at[t, k, way, hop - 1], (frm, j), cond)
            if hop < half:
                onward = both(needed(t, row, col), reach(way, hop + 1, parity))
                send(slot, slot, ring_s.at[t, k, way, hop], ring_r.at[t, k, way, hop], (to, j), onward)
            if t == 2:
                send(slot, slot, late_s.at[way, hop], late_r.at[way, hop], (i, across), cond)
            send(slot, slot, side_s.at[t, k, way, hop], side_r.at[t, k, way, hop], (i, beside), cond)

    def side_arrivals(t, k):
        col = guests[k]
        for hop in range(half + 1):
            for way in (0, 1):
                if hop == 0 and way == 1:
                    continue
                row = i if hop == 0 else (member(pos - hop) if way == 0 else member(pos + hop))
                limit = None if hop == 0 else reach(way, hop, 1 - parity)
                receive(bufs[t].at[row, col], side_s.at[t, k, way, hop], side_r.at[t, k, way, hop], (i, beside), both(needed(t, row, col), limit))

    def exchange(t):
        slot = bufs[t].at[i, j]
        send(slot, slot, cross_s.at[t], cross_r.at[t], (i, across), needed(t, i, j))

    def exchanged(t):
        receive(bufs[t].at[i, across], cross_s.at[t], cross_r.at[t], (i, across), needed(t, i, across))

    chunk = pick_ref.shape[1]
    mine = pl.ds(pl.multiple_of(j * chunk, chunk), chunk)
    own = gm.at[i, j]
    more = ge.at[i, j]
    own[:, :cols] = jnp.where(i // ratio > j, l_ref[...], u_ref[...])
    own[:, cols:] = b_ref[:, mine]

    @pl.when(i // ratio == j)
    def _():
        at = pl.multiple_of((i % ratio) * BLOCK, BLOCK)
        more[...] = l_ref[...]
        own[:, pl.ds(at, BLOCK)] = inverse(u_ref[:, pl.ds(at, BLOCK)], True)
        more[:, pl.ds(at, BLOCK)] = inverse(l_ref[:, pl.ds(at, BLOCK)], False)

    pl.semaphore_wait(barrier, n + m - 2)
    exchange(0)
    exchange(1)
    emit(0, 0)
    emit(1, 0)
    coup_ref[...] = dot3(split(vb_ref[...]), split(lb_ref[...]), TN)
    for d in range(1, n):
        to = (i + d) % n
        send(coup_ref.at[pl.ds(to * crow, crow)], cslots.at[d - 1], sum_s.at[d - 1], sum_r.at[d - 1], (to, j))
    exchanged(0)
    exchanged(1)
    emit(0, 1)
    emit(1, 1)
    gu[j] = up_ref[...]
    send(gu.at[j], gu.at[j], up_s.at[0], up_r.at[0], (i, across))
    send(gu.at[j], gu.at[j], up_s.at[1], up_r.at[1], (i, beside))
    for t in (0, 1):
        for k in (0, 1):
            advance(t, k, 1)
    pick_rows(i, vb_ref, piv_ref, pick_ref, mine)
    for t in (0, 1):
        for k in (0, 1):
            advance(t, k, 2)
    total = coup_ref[pl.ds(i * crow, crow), :]
    for d in range(1, n):
        receive(cslots.at[d - 1], sum_s.at[d - 1], sum_r.at[d - 1], ((i - d + n) % n, j))
        total = total + cslots[d - 1]
    gc[i, j] = total
    emit(2, 0)
    for t in (0, 1):
        for k in (0, 1):
            advance(t, k, 3)
    advance(2, 0, 1)
    for d in range(1, n):
        to = (i + d) % n
        send(pick_ref.at[pl.ds(to * rows, rows)], xslots.at[d - 1], pick_s.at[d - 1], pick_r.at[d - 1], (to, j))
    for t in (0, 1):
        for k in (0, 1):
            advance(t, k, half)
    advance(2, 0, 2)
    crossed(0)
    for t in (0, 1):
        for k in (0, 1):
            side_arrivals(t, k)
    assemble(n, m, gm, ge, uh, ul, lh, ll, bs)
    advance(2, 0, 3)
    crossed(1)
    receive(gu.at[across], up_s.at[0], up_r.at[0], (i, across))
    send(gu.at[across], gu.at[across], up_s.at[2], up_r.at[2], (i, beside))

    def service(p):
        if p == 1:
            advance(2, 0, half)
        if p in (2, 4, 6):
            crossed(p // 2 + 1)

    first_solve(bs, cs, wh, wl, uh, ul, service)
    own = pick_ref[pl.ds(i * rows, rows), :]
    for d in range(1, n):
        receive(xslots.at[d - 1], pick_s.at[d - 1], pick_r.at[d - 1], ((i - d + n) % n, j))
        own = own + xslots[d - 1]
    xparts[j] = own
    for d in range(1, m):
        send(xparts.at[j], xparts.at[j], x_s.at[d - 1], x_r.at[d - 1], (i, (j + d) % m))
    receive(gu.at[beside], up_s.at[1], up_r.at[1], (i, beside))
    receive(gu.at[guests[1]], up_s.at[2], up_r.at[2], (i, beside))
    rest_update(wh, wl, lambda ts: jnp.concatenate([gu[q, :, ts] for q in range(m)], axis=0), br_ref, wr_ref)
    for k in (0, 1):
        side_arrivals(2, k)
    for a in range(n):
        for b in range(m):
            cs[a * crow : (a + 1) * crow, b * cols : (b + 1) * cols] -= gc[a, b]
    second_solve(cs, wh, wl, lh, ll)
    interchange(i, wh, wl, vb_ref, piv_ref, xr_ref)
    for d in range(1, m):
        frm = (j - d + m) % m
        receive(xparts.at[frm], x_s.at[d - 1], x_r.at[d - 1], (i, frm))
    for q in range(m):
        xp[:, q * chunk : (q + 1) * chunk] = xparts[q]
    for cond, copy in pending:
        guard(cond, copy.wait_send)


def main_kernel(pre, g_ref, e_ref, c_ref, up_ref, br_ref, vb_ref, piv_ref, wr_ref, xr_ref, uh, ul, lh, ll, bs, cs, wh, wl):
    n_row, n_col, crow, cols = c_ref.shape
    assemble(n_row, n_col, g_ref, e_ref, uh, ul, lh, ll, bs)
    if not pre:
        for p in range(uh.shape[0] // BLOCK):
            sl = slice(p * BLOCK, (p + 1) * BLOCK)
            uh[sl, sl], ul[sl, sl] = split(inverse(uh[sl, sl].astype(F32) + ul[sl, sl].astype(F32), True))
            lh[sl, sl], ll[sl, sl] = split(inverse(lh[sl, sl].astype(F32) + ll[sl, sl].astype(F32), False))
    first_solve(bs, cs, wh, wl, uh, ul, lambda p: None)
    for a in range(n_row):
        for b in range(n_col):
            cs[a * crow : (a + 1) * crow, b * cols : (b + 1) * cols] -= c_ref[a, b]
    rest_update(wh, wl, lambda ts: up_ref[:, ts], br_ref, wr_ref)
    second_solve(cs, wh, wl, lh, ll)
    interchange(lax.axis_index("prow"), wh, wl, vb_ref, piv_ref, xr_ref)


def body(n_row, n_col, b_panel, b_rest, u_diag, u_panel, l_diag, l_below, v_below, pivot):
    rows, cols = u_diag.shape
    total, rhs = pivot.shape[0], b_panel.shape[1]
    chunk = rhs // n_col
    pre = rows == BLOCK
    piv = pivot[None, :]
    vm = pl.BlockSpec(memory_space=pltpu.VMEM)
    params = pltpu.CompilerParams(vmem_limit_bytes=56 << 20)
    halves = [pltpu.VMEM((total, total), BF16)] * 4
    halves += [pltpu.VMEM((total, rhs), F32), pltpu.VMEM((rhs, total), F32)]
    halves += [pltpu.VMEM((rhs, total), BF16)] * 2
    if pre and n_row == 8 and n_col == 4:
        crow, half = rhs // n_row, n_row // 2
        shapes = [(3, 2, 2, half), (3, 2, 2, half + 1), (2,), (n_row - 1,), (n_row - 1,), (n_col - 1,), (3,), (2, half + 1)]
        w_rest, x_rest, x_panel = pl.pallas_call(
            functools.partial(whole_kernel, n_row, n_col),
            out_shape=(
                jax.ShapeDtypeStruct(b_rest.shape, F32),
                jax.ShapeDtypeStruct(v_below.shape, F32),
                jax.ShapeDtypeStruct((rows, rhs), F32),
            ),
            in_specs=[vm] * 8,
            out_specs=(vm,) * 3,
            scratch_shapes=[
                pltpu.VMEM((n_row, n_col, rows, cols + chunk), F32),
                pltpu.VMEM((n_row, n_col, rows, cols), F32),
                pltpu.VMEM((n_row, n_col, crow, cols), F32),
                pltpu.VMEM((n_col,) + u_panel.shape, F32),
                pltpu.VMEM((rhs, cols), F32),
                pltpu.VMEM((total, chunk), F32),
            ]
            + halves
            + [
                pltpu.VMEM((n_row - 1, crow, cols), F32),
                pltpu.VMEM((n_row - 1, rows, chunk), F32),
                pltpu.VMEM((n_col, rows, chunk), F32),
            ]
            + [pltpu.SemaphoreType.DMA(shape) for shape in shapes for _ in range(2)],
            compiler_params=pltpu.CompilerParams(vmem_limit_bytes=60 << 20, collective_id=0, has_side_effects=True),
        )(u_diag, l_diag, b_panel, l_below, v_below, piv, u_panel, b_rest)
        return w_rest, x_panel, x_rest
    pack, extra, coup, pick = pl.pallas_call(
        functools.partial(prep_kernel, pre),
        out_shape=(
            jax.ShapeDtypeStruct((rows, cols + chunk), F32),
            jax.ShapeDtypeStruct((rows, cols), F32),
            jax.ShapeDtypeStruct((rhs, cols), F32),
            jax.ShapeDtypeStruct((total, chunk), F32),
        ),
        in_specs=[vm] * 6,
        out_specs=(vm,) * 4,
        compiler_params=params,
    )(u_diag, l_diag, b_panel, l_below, v_below, piv)

    def everywhere(piece):
        return lax.all_gather(piece, ("prow", "pcol"), axis=0).reshape((n_row, n_col) + piece.shape)

    upan = lax.all_gather(u_panel, "pcol", axis=0, tiled=True)
    csum = lax.psum_scatter(coup, "prow", scatter_dimension=0, tiled=True)
    xsum = lax.psum_scatter(pick, "prow", scatter_dimension=0, tiled=True)
    x_panel = lax.all_gather(xsum, "pcol", axis=1, tiled=True)
    w_rest, x_rest = pl.pallas_call(
        functools.partial(main_kernel, pre),
        out_shape=(jax.ShapeDtypeStruct(b_rest.shape, F32), jax.ShapeDtypeStruct(v_below.shape, F32)),
        in_specs=[vm] * 7,
        out_specs=(vm, vm),
        scratch_shapes=halves,
        compiler_params=params,
    )(everywhere(pack), everywhere(extra), everywhere(csum), upan, b_rest, v_below, piv)
    return w_rest, x_panel, x_rest


def solution(mesh):
    in_specs = (
        P("prow", None),
        P("prow", None),
        P("prow", "pcol"),
        P("pcol", "prow"),
        P("prow", "pcol"),
        P("prow", "pcol"),
        P("prow", None),
        P(),
    )
    out_specs = (P("prow", None), P("prow", None), P("prow", None))
    step = functools.partial(body, mesh.shape["prow"], mesh.shape["pcol"])
    return jax.shard_map(step, mesh=mesh, in_specs=in_specs, out_specs=out_specs, check_vma=False)
```

time: 130 us -> 105 us (0.81)
  Pallas kernels: 128 us -> 99.2 us
  local copies, waits for them, and re-layouts: 0.71 us -> 5.26 us
    pallas_call x3 -> x1, Pallas kernels: 128 us -> 99.2 us  [body(): pl.pallas_call(functools.partial(whole_kernel, n_row, n_col), out_shape=(...]
    unnamed x3 -> x7, local copies, waits for them, and re-layouts: 0.71 us -> 5.26 us
where the time goes in v2:
time: 105 us
  Pallas kernels  99.2 us (94%)
  local copies, waits for them, and re-layouts  5.26 us (5%)
    pallas_call x1, Pallas kernels, body(): pl.pallas_call(functools.partial(whole_kernel, n_row, n_col), out_shape=(...  99.2 us
    unnamed x7, local copies, waits for them, and re-layouts  5.26 us

profile of v2, /device:TPU:0, one launch (start us, length us, event | category | flops | bytes accessed | tf_op | source)
XLA Modules:
  0.0 105.1 jit_solution(12106171446651770560)
XLA Ops:
  0.6 99.2 %shard_map.103 = (f32[1024,512]{1,0:T(8,128)}, f32[1024,512]{1,0:T(8,128)}, f32[128,512]{1,0:T(8,128)}) custom-call(f32[128,256]{1,0:T(8,128)} %u_ref.1, f32[128,256]{1,0:T(8,128)} %l_ref.1, f32[128,512]{1,0:T(8,128)} %b_ref.1, f32[1024,256]{1,0:T(8,128)} %lb_ref.1, f32[1024,512]{1,0:T(8,128)} %vb_ref.1, s32[1,1024]{1,0:T(1,128)} %bitcast.1, ...), custom_call_target="tpu_custom_call" | custom-call | tf_op jit(solution)/shard_map/pallas_call | solution.py:392
  99.8 0.0 copy-start.1
  99.8 0.0 copy-start
  99.8 3.2 %copy.14 = f32[1024,512]{1,0:T(8,128)} copy(f32[1024,512]{1,0:T(8,128)} %get-tuple-element.12) | data formatting | bytes 4194304
  103.0 0.0 copy-done.1
  103.0 0.7 copy.15
  103.8 0.0 copy-done
  103.8 1.3 %copy.16 = f32[1024,512]{1,0:T(8,128)} copy(f32[1024,512]{1,0:T(8,128)S(1)} %copy-done) | data formatting | bytes 4194304
Async XLA Ops:
  99.8 3.3 %copy-start.1 = (f32[128,512]{1,0:T(8,128)S(1)}, f32[128,512]{1,0:T(8,128)}, u32[]{:S(2)}) copy-start(f32[128,512]{1,0:T(8,128)} %get-tuple-element.13) | copy-start | bytes 786436
  99.8 3.9 %copy-start = (f32[1024,512]{1,0:T(8,128)S(1)}, f32[1024,512]{1,0:T(8,128)}, u32[]{:S(2)}) copy-start(f32[1024,512]{1,0:T(8,128)} %get-tuple-element.14) | copy-start | bytes 6291460

commit v3 on v2

--- a/solution.py
+++ b/solution.py
@@ -308,9 +308,6 @@
         for k in (0, 1):
             advance(t, k, 3)
     advance(2, 0, 1)
-    for d in range(1, n):
-        to = (i + d) % n
-        send(pick_ref.at[pl.ds(to * rows, rows)], xslots.at[d - 1], pick_s.at[d - 1], pick_r.at[d - 1], (to, j))
     for t in (0, 1):
         for k in (0, 1):
             advance(t, k, half)
@@ -319,6 +316,9 @@
     for t in (0, 1):
         for k in (0, 1):
             side_arrivals(t, k)
+    for d in range(1, n):
+        to = (i + d) % n
+        send(pick_ref.at[pl.ds(to * rows, rows)], xslots.at[d - 1], pick_s.at[d - 1], pick_r.at[d - 1], (to, j))
     assemble(n, m, gm, ge, uh, ul, lh, ll, bs)
     advance(2, 0, 3)
     crossed(1)

time: 105 us -> 105 us (level)
  no operation moved by 1% of the time
where the time goes in v3:
time: 105 us; the launch traced here: 104 us
  Pallas kernels  98.5 us (94%)
  local copies, waits for them, and re-layouts  5.26 us (5%)
    pallas_call x1, Pallas kernels, body(): pl.pallas_call(functools.partial(whole_kernel, n_row, n_col), out_shape=(...  98.5 us
    unnamed x7, local copies, waits for them, and re-layouts  5.26 us

profile of v3, /device:TPU:0, one launch (start us, length us, event | category | flops | bytes accessed | tf_op | source)
XLA Modules:
  0.0 104.4 jit_solution(17887517773671506551)
XLA Ops:
  0.6 98.5 %shard_map.103 = (f32[1024,512]{1,0:T(8,128)}, f32[1024,512]{1,0:T(8,128)}, f32[128,512]{1,0:T(8,128)}) custom-call(f32[128,256]{1,0:T(8,128)} %u_ref.1, f32[128,256]{1,0:T(8,128)} %l_ref.1, f32[128,512]{1,0:T(8,128)} %b_ref.1, f32[1024,256]{1,0:T(8,128)} %lb_ref.1, f32[1024,512]{1,0:T(8,128)} %vb_ref.1, s32[1,1024]{1,0:T(1,128)} %bitcast.1, ...), custom_call_target="tpu_custom_call" | custom-call | tf_op jit(solution)/shard_map/pallas_call | solution.py:392
  99.1 0.0 copy-start.1
  99.1 0.0 copy-start
  99.1 3.2 %copy.14 = f32[1024,512]{1,0:T(8,128)} copy(f32[1024,512]{1,0:T(8,128)} %get-tuple-element.12) | data formatting | bytes 4194304
  102.4 0.0 copy-done.1
  102.4 0.7 copy.15
  103.1 0.0 copy-done
  103.1 1.3 %copy.16 = f32[1024,512]{1,0:T(8,128)} copy(f32[1024,512]{1,0:T(8,128)S(1)} %copy-done) | data formatting | bytes 4194304
Async XLA Ops:
  99.1 3.3 %copy-start.1 = (f32[128,512]{1,0:T(8,128)S(1)}, f32[128,512]{1,0:T(8,128)}, u32[]{:S(2)}) copy-start(f32[128,512]{1,0:T(8,128)} %get-tuple-element.13) | copy-start | bytes 786436
  99.1 3.9 %copy-start = (f32[1024,512]{1,0:T(8,128)S(1)}, f32[1024,512]{1,0:T(8,128)}, u32[]{:S(2)}) copy-start(f32[1024,512]{1,0:T(8,128)} %get-tuple-element.14) | copy-start | bytes 6291460
